TPU v7x, 768 devices: a whole 4x8x12 slice. The times are simulated.
768 devices in a mesh: band: 12 (over z_lo, core), col: 64 (over x, y, z_hi).
Axes of the slice: x: 4, y: 8, z: 12 (z_hi: 2, z_lo: 6; z = z_hi * 6 + z_lo), core: 2. Of those that a mesh axis runs over, the one named last changes fastest.
Arguments:
- adjoint_tend: bfloat16 [64, 40, 12, 5120], P('col', None, 'band'), may hold values from -6 to 6
- trajectory: bfloat16 [40, 12, 5120], P(None, 'band', 'col'), may hold values from -3 to 3
- coupling: bfloat16 [40, 40], replicated, may hold values from -1 to 1
- row_lat: int32 [12], P('band'), may hold values from 0 to 2559, as said below
- row_points: int32 [12], P('band'), may hold values from 20 to 5120, as said below
- wave_order: int32 [768], replicated, may hold values from 0 to 767, each once
Outputs:
- spectra: bfloat16 [64, 2, 40, 12, 768], P('col', None, None, None, 'band')
Inputs may be any that keep to these rules, and one draw needn't show every extreme that they name: `row_lat`: latitude rows are counted from the north pole. `row_points`: the row of latitude index i has min(20 + 4 d, 5120) points, d = min(i, 2559 - i), placed at point indices 0 to that number minus one; the rest of the row slot is unused.
All inputs are finite; a program needn't handle non-finite values.
Results may differ from a plain program's by a relative error of at most 0.0055.
Values may be sent and summed in bfloat16 or wider, within the bound.
A program may use at most 64 MiB of HBM per device.

v0:
```python
import math

import jax
import jax.numpy as jnp
from jax import lax
from jax.sharding import PartitionSpec as P

LEVELS = 8
LATITUDES = 2560


def latitude_factor(row_lat):
    ratio = (2.0 * row_lat.astype(jnp.float32) + 1.0) / LATITUDES
    return jnp.sin(0.5 * math.pi * (1.0 - ratio))


def grid_adjoint(tend_block, traj_block, coupling, coriolis, row_points, first_point):
    width = tend_block.shape[3]
    driven = jnp.einsum("ab,brp->arp", coupling, traj_block, preferred_element_type=jnp.float32)
    tend_wide = tend_block.astype(jnp.float32)
    weighted = tend_wide * (1.0 + traj_block.astype(jnp.float32))[None]
    backed = jnp.einsum(
        "ab,karp->kbrp", coupling.astype(jnp.float32), weighted, precision=lax.Precision.HIGHEST
    )
    total = backed + tend_wide * driven[None]
    turning = coriolis[None, None, :, None]
    eastward = tend_wide[:, :LEVELS]
    northward = tend_wide[:, LEVELS : 2 * LEVELS]
    total = jnp.concatenate(
        [
            total[:, :LEVELS] - turning * northward,
            total[:, LEVELS : 2 * LEVELS] + turning * eastward,
            total[:, 2 * LEVELS :],
        ],
        axis=1,
    )
    places = first_point + jnp.arange(width, dtype=jnp.int32)
    keep = places[None, :] < row_points[:, None]
    return jnp.where(keep[None, None], total, 0.0).astype(jnp.bfloat16)


def wave_table(points, waves, width):
    places = jnp.arange(width, dtype=jnp.int32)
    phase = places[:, None] * waves[None, :] % points
    angle = phase.astype(jnp.float32) * (2.0 * math.pi) / points.astype(jnp.float32)
    keep = (2 * waves < points)[None, :]
    cosine = jnp.where(keep, jnp.cos(angle), 0.0)
    sine = jnp.where(keep, -jnp.sin(angle), 0.0)
    return jnp.concatenate([cosine, sine], axis=1).astype(jnp.bfloat16)


def body(adjoint_tend, trajectory, coupling, row_lat, row_points, wave_order):
    coriolis = latitude_factor(row_lat)
    members = adjoint_tend.shape[0]
    column_vars = adjoint_tend.shape[1]
    spread = lax.all_to_all(adjoint_tend, "col", split_axis=3, concat_axis=0, tiled=True)
    first_point = lax.axis_index("col") * trajectory.shape[2]
    grid_local = grid_adjoint(spread, trajectory, coupling, coriolis, row_points, first_point)
    grid = lax.all_to_all(grid_local, "col", split_axis=0, concat_axis=3, tiled=True)
    width = grid.shape[3]
    waves_total = wave_order.shape[0]
    block = math.gcd(waves_total, 256)
    points = row_points[0]
    flat = grid[:, :, 0, :].reshape(members * column_vars, width)
    root = jnp.sqrt(points.astype(jnp.float32))
    cosines = []
    sines = []
    for first_wave in range(0, waves_total, block):
        table = wave_table(points, wave_order[first_wave : first_wave + block], width)
        coeffs = jnp.dot(flat, table, preferred_element_type=jnp.float32) / root
        cosines.append(coeffs[:, :block])
        sines.append(coeffs[:, block:])
    real_part = (
        jnp.concatenate(cosines, axis=1)
        .astype(jnp.bfloat16)
        .reshape(members, column_vars, waves_total)
    )
    imag_part = (
        jnp.concatenate(sines, axis=1)
        .astype(jnp.bfloat16)
        .reshape(members, column_vars, waves_total)
    )
    per_row = [jnp.stack([real_part, imag_part], axis=1)]
    spectra = jnp.stack(per_row, axis=3)
    return lax.all_to_all(spectra, "band", split_axis=4, concat_axis=3, tiled=True)


def solution(mesh):
    return jax.shard_map(
        body,
        mesh=mesh,
        in_specs=(
            P("col", None, "band", None),
            P(None, "band", "col"),
            P(),
            P("band"),
            P("band"),
            P(),
        ),
        out_specs=P("col", None, None, None, "band"),
        check_vma=False,
    )
```

profile of v0, /device:TPU:1, one launch (start us, length us, event | category | flops | bytes accessed | tf_op | source)
XLA Modules:
  0.0 333.5 jit_solution(5655007725931010050)
XLA Ops:
  0.0 4.3 %copy.22 = bf16[1,40,1,5120]{1,2,0,3:T(2,128)(2,1)S(1)} copy(bf16[1,40,1,5120]{3,1,2,0:T(8,128)(2,1)} %param.6) | data formatting | bytes 819200 | tf_op args[0]
  4.3 0.5 broadcast.80
  4.8 28.9 %reduce = bf16[5120,40]{1,0:T(8,128)(2,1)} reduce(bf16[5120,1,1,40]{3,2,1,0:T(2,128)(2,1)S(1)} %bitcast.68, bf16[]{:T(256)} %broadcast.80), dimensions={1,2}, to_apply=%bitcast.54.reduce_sub_computation | reduce | bytes 819202
  33.8 3.8 %reshape.209 = bf16[64,2,1600]{2,1,0:T(2,128)(2,1)} reshape(bf16[5120,40]{1,0:T(8,128)(2,1)} %reduce) | data formatting | bytes 819200
  37.6 24.0 %all-to-all-start = ((bf16[64,2,1600]{2,1,0:T(2,128)(2,1)}), bf16[64,2,1600]{2,1,0:T(2,128)(2,1)S(1)}, u32[]{:S(2)}, u32[]{:S(2)}) async-start(bf16[64,2,1600]{2,1,0:T(2,128)(2,1)} %reshape.209), calls=%async_computation | async-start | bytes 851968 | tf_op jit(solution)/shard_map/all_to_all | solution.py:56
  61.6 0.1 fusion.58
  63.2 143.3 %select_convert_fusion.1 = (bf16[5120,256]{1,0:T(8,128)(2,1)}, bf16[5120,256]{1,0:T(8,128)(2,1)}, bf16[5120,256]{1,0:T(8,128)(2,1)}, bf16[5120,256]{1,0:T(8,128)(2,1)}) fusion(pred[256]{0:T(512)(128)(4,1)S(1)} %get-tuple-element.15, f32[]{:T(128)S(6)} %convert_element_type.95, pred[]{:T(512)S(6)} %lt.52, s32[]{:T(128)S(6)} %select_n.49, ...), kind=kLoop, calls=%fused_computation.25 | loop fusion | flops 41943040 | bytes 10488329 | tf_op jit(solution)/shard_map/convert.24
  206.5 0.0 all-to-all-done
  206.5 2.3 reshape.210
  208.8 1.4 copy.23
  210.3 0.7 reshape.206
  211.0 0.8 copy.42
  211.8 2.4 fusion.33
  214.2 0.1 slice.66
  214.2 0.1 fusion.57
  214.3 1.0 fusion.54
  215.3 17.0 %all-to-all-start.1 = ((bf16[64,40,1,80]{3,1,2,0:T(8,128)(2,1)}), bf16[64,40,1,80]{3,1,2,0:T(8,128)(2,1)S(1)}, u32[]{:S(2)}, u32[]{:S(2)}) async-start(bf16[64,40,1,80]{3,1,2,0:T(8,128)(2,1)} %fusion.54), calls=%async_computation.1 | async-start | bytes 1310720 | tf_op jit(solution)/shard_map/all_to_all | solution.py:59
  232.3 71.8 %select_convert_fusion.5 = (bf16[5120,256]{1,0:T(8,128)(2,1)}, bf16[5120,256]{1,0:T(8,128)(2,1)}) fusion(f32[]{:T(128)S(6)} %convert_element_type.95, pred[]{:T(512)S(6)} %lt.52, s32[]{:T(128)S(6)} %select_n.49, s32[256]{0:T(256)S(1)} %get-tuple-element.16, pred[256]{0:T(512)(128)(4,1)S(1)} %get-tuple-element.13), kind=kLoop, calls=%fused_computation.35 | loop fusion | flops 20971520 | bytes 5244169 | tf_op jit(solution)/shard_map/convert.28
  304.2 0.0 all-to-all-done.1
  304.2 0.1 copy.27
  304.3 1.2 reshape_squeeze.3
  305.5 3.6 %fusion.39 = bf16[40,512]{1,0:T(8,128)(2,1)S(1)} fusion(bf16[40,5120]{1,0:T(8,128)(2,1)S(1)} %reshape_squeeze.3, bf16[5120,256]{1,0:T(8,128)(2,1)} %get-tuple-element.24, bf16[5120,256]{1,0:T(8,128)(2,1)} %get-tuple-element.23, f32[]{:T(128)S(6)} %sqrt.3), kind=kOutput, calls=%fused_computation.53 | convolution fusion | flops 220241920 | bytes 5693444 | tf_op jit(solution)/shard_map/dot_general | solution.py:70
  309.2 0.4 copy-done.4
  309.6 1.0 fusion.45
  310.6 0.7 copy-done.1
  311.3 0.8 copy-done.2
  312.1 1.0 fusion.51
  313.2 0.4 copy.28
  313.6 0.6 reshape.211
  314.2 17.7 %all_to_all.36 = bf16[12,2,2560]{2,1,0:T(2,128)(2,1)S(1)} all-to-all(bf16[12,2,2560]{2,1,0:T(2,128)(2,1)S(1)} %reshape.211), channel_id=1, replica_groups=mesh['band'=12,'col'=64] {'band'}, dimensions={0} | all-to-all | bytes 245760 | tf_op jit(solution)/shard_map/all_to_all | solution.py:85
  331.9 0.6 reshape.212
  332.5 1.0 copy.30
  (19 shorter events, 0.1 us)
Async XLA Ops:
  0.0 61.6 %copy-start = (bf16[40,40]{1,0:T(8,128)(2,1)S(1)}, bf16[40,40]{1,0:T(8,128)(2,1)}, u32[]{:S(2)}) copy-start(bf16[40,40]{1,0:T(8,128)(2,1)} %param.8) | copy-start | bytes 9604
  4.8 56.7 %copy-start.5 = (bf16[40,1,80]{2,0,1:T(8,128)(2,1)S(1)}, bf16[40,1,80]{2,0,1:T(8,128)(2,1)}, u32[]{:S(2)}) copy-start(bf16[40,1,80]{2,0,1:T(8,128)(2,1)} %param.7) | copy-start | bytes 19204
  4.8 58.3 %copy-start.6 = (s32[768]{0:T(1024)S(1)}, s32[768]{0:T(1024)}, u32[]{:S(2)}) copy-start(s32[768]{0:T(1024)} %param.11) | copy-start | bytes 9220
  37.6 169.0 %all-to-all-start = ((bf16[64,2,1600]{2,1,0:T(2,128)(2,1)}), bf16[64,2,1600]{2,1,0:T(2,128)(2,1)S(1)}, u32[]{:S(2)}, u32[]{:S(2)}) async-start(bf16[64,2,1600]{2,1,0:T(2,128)(2,1)} %reshape.209), calls=%async_computation | async-start | bytes 851968 | tf_op jit(solution)/shard_map/all_to_all | solution.py:56
  215.3 88.9 %all-to-all-start.1 = ((bf16[64,40,1,80]{3,1,2,0:T(8,128)(2,1)}), bf16[64,40,1,80]{3,1,2,0:T(8,128)(2,1)S(1)}, u32[]{:S(2)}, u32[]{:S(2)}) async-start(bf16[64,40,1,80]{3,1,2,0:T(8,128)(2,1)} %fusion.54), calls=%async_computation.1 | async-start | bytes 1310720 | tf_op jit(solution)/shard_map/all_to_all | solution.py:59
  305.5 3.7 %copy-start.3 = (bf16[5120,256]{1,0:T(8,128)(2,1)S(1)}, bf16[5120,256]{1,0:T(8,128)(2,1)}, u32[]{:S(2)}) copy-start(bf16[5120,256]{1,0:T(8,128)(2,1)} %get-tuple-element.25) | copy-start | bytes 7864324
  305.5 4.1 %copy-start.4 = (bf16[5120,256]{1,0:T(8,128)(2,1)S(1)}, bf16[5120,256]{1,0:T(8,128)(2,1)}, u32[]{:S(2)}) copy-start(bf16[5120,256]{1,0:T(8,128)(2,1)} %get-tuple-element.26) | copy-start | bytes 7864324
  309.6 1.7 copy-start.1
  309.6 2.5 copy-start.2
where the time goes:
time: 334 us
  other arithmetic  245 us (73%)
  starting transfers between devices  41 us (12%)
  local copies, waits for them, and re-layouts  19.7 us (6%)
  blocking collectives  17.7 us (5%)
  matrix products  8.17 us (2%)
    another operation x2, other arithmetic  215 us
    unnamed x1, other arithmetic  28.9 us
    all_to_all x1, starting transfers between devices, body(): lax.all_to_all(adjoint_tend, 'col', split_axis=3, concat_axis=0, tiled=True)  24 us
    all_to_all x1, blocking collectives, body(): lax.all_to_all(spectra, 'band', split_axis=4, concat_axis=3, tiled=True)  17.7 us
    all_to_all x1, starting transfers between devices, body(): lax.all_to_all(grid_local, 'col', split_axis=0, concat_axis=3, tiled=True)  17 us
    unnamed x20, local copies, waits for them, and re-layouts  14 us
  transfers between devices with their start and end apart: 2, of which 0 were waited for; matrix products, arithmetic and copies ran while one was open for 65% of the time, Pallas kernels for 0%

commit v1 on v0

v1 whole, which is shorter than its diff:
```python
import jax
import jax.numpy as jnp
from jax import lax
from jax.experimental import pallas as pl
from jax.experimental.pallas import tpu as pltpu
from jax.sharding import PartitionSpec as P

LEVELS = 8
LATITUDES = 2560
VARS = 40
POINTS = 5120
PIECE = 80
COLS = 64
BANDS = 12
OWN_WAVES = 64
LANES = 2 * BANDS * OWN_WAVES
FINE = 256
COARSE = POINTS // FINE
SINE = (6.283185005187988, -41.34165573120117, 81.60100555419922, -76.5497817993164, 39.536705017089844)


def sine_turns(v):
    u = v * v
    p = jnp.full_like(u, SINE[-1])
    for c in SINE[-2::-1]:
        p = p * u + c
    return p * v


def cosine_turns(t):
    v = 0.25 - jnp.abs(t)
    return sine_turns(jnp.maximum(v, -0.5 - v))


def turns(pm, n, rn):
    q = jnp.floor(pm * rn + 0.5)
    return (pm - q * n) * rn


def tables(pts_ref, waves_ref, fine_ref, a_ref, b_ref):
    points = pts_ref[0].astype(jnp.float32)
    lane = lax.broadcasted_iota(jnp.int32, (8, 128), 1)
    first_half = lane < 64
    n8 = jnp.full((8, 128), points, jnp.float32)
    rn8 = 1.0 / n8
    root8 = 1.0 / jnp.sqrt(n8)
    shift8 = jnp.where(first_half, 0.0, 0.25)
    sign8 = jnp.where(first_half, 1.0, -1.0)
    for tile in range(6):
        pair = jnp.broadcast_to(waves_ref[:, 128 * tile : 128 * tile + 128], (8, 128)).astype(jnp.float32)
        turned = pltpu.roll(pair, 64, 1)
        for odd in range(2):
            w8 = jnp.where(first_half, pair, turned) if odd == 0 else jnp.where(first_half, turned, pair)
            at = (2 * tile + odd) * 128
            scale = jnp.where(2.0 * w8 < n8, root8, 0.0)
            for k in range(3):
                p1 = lax.broadcasted_iota(jnp.int32, (8, 128), 0).astype(jnp.float32) + 8.0 * k
                t = turns(p1 * FINE * w8, n8, rn8)
                a_ref[8 * k : 8 * k + 8, at : at + 128] = scale * sign8 * cosine_turns(t)
                b_ref[8 * k : 8 * k + 8, at : at + 128] = -scale * cosine_turns(t - 0.25)
            wide = lambda v: jnp.broadcast_to(v[None], (FINE // 8, 8, 128)).reshape(FINE, 128)
            p0 = lax.broadcasted_iota(jnp.int32, (FINE, 128), 0).astype(jnp.float32)
            t = turns(p0 * wide(w8), wide(n8), wide(rn8))
            fine_ref[:, at : at + 128] = cosine_turns(t - wide(shift8)).astype(jnp.bfloat16)


def joined(pieces):
    lane = lax.broadcasted_iota(jnp.int32, (VARS, 128), 1)
    tiles = [None] * 5
    for j, piece in enumerate(pieces):
        tile, at = divmod(PIECE * j, 128)
        turned = piece if at == 0 else pltpu.roll(piece, at, 1)
        tiles[tile] = turned if tiles[tile] is None else jnp.where(lane < at, tiles[tile], turned)
        if at + PIECE > 128:
            tiles[tile + 1] = turned
    return jnp.concatenate(tiles, axis=1)


def column(lat_ref, pts_ref, tend_ref, piece_of, coup_ref, x_ref):
    ratio = (2.0 * jnp.full((8, 128), lat_ref[0].astype(jnp.float32)) + 1.0) / LATITUDES
    turning = jnp.tile(sine_turns(0.25 - 0.25 * ratio), (1, 5))
    coup = coup_ref[...]
    back = coup.astype(jnp.float32).T.astype(jnp.bfloat16)
    back2 = jnp.concatenate([back, back], axis=1)
    points = pts_ref[0]
    place = lax.broadcasted_iota(jnp.int32, (VARS, 640), 1)

    def run(g):
        at = g * 640
        traj = joined([piece_of(8 * g + j).astype(jnp.float32) for j in range(8)])
        tend = tend_ref[:, pl.ds(pl.multiple_of(at, 128), 640)].astype(jnp.float32)
        driven = jnp.dot(coup, traj.astype(jnp.bfloat16), preferred_element_type=jnp.float32)
        weighted = tend * (1.0 + traj)
        high = weighted.astype(jnp.bfloat16).astype(jnp.float32)
        both = jnp.concatenate([high, weighted - high], axis=0).astype(jnp.bfloat16)
        backed = jnp.dot(back2, both, preferred_element_type=jnp.float32)
        total = backed + tend * driven
        total = jnp.concatenate(
            [
                total[:LEVELS] - turning * tend[LEVELS : 2 * LEVELS],
                total[LEVELS : 2 * LEVELS] + turning * tend[:LEVELS],
                total[2 * LEVELS :],
            ],
            axis=0,
        )
        return jnp.where(place < points - at, total, 0.0)

    def two_runs(i, carry):
        for half in range(2):
            total = run(2 * i + half)
            for k in range(5):
                tile = 5 * half + k
                x_ref[5 * i + tile // 2, :, 128 * (tile % 2) : 128 * (tile % 2) + 128] = total[:, 128 * k : 128 * k + 128]
        return carry

    lax.fori_loop(0, 4, two_runs, 0)


def transform(x_ref, x16_ref, fine_ref, a_ref, b_ref, put):
    x16_ref[...] = x_ref[...].reshape(COARSE * VARS, FINE).astype(jnp.bfloat16)

    def block(j, carry):
        at = pl.multiple_of(j * 256, 256)
        y = jnp.dot(x16_ref[...], fine_ref[:, pl.ds(at, 256)], preferred_element_type=jnp.float32)
        u = jnp.zeros((VARS, 256), jnp.float32)
        v = jnp.zeros((VARS, 256), jnp.float32)
        for p1 in range(COARSE):
            part = y[VARS * p1 : VARS * (p1 + 1)]
            u = u + part * a_ref[p1 : p1 + 1, pl.ds(at, 256)]
            v = v + part * b_ref[p1 : p1 + 1, pl.ds(at, 256)]
        for odd in range(2):
            half = slice(128 * odd, 128 * odd + 128)
            put(2 * j + odd, (u[:, half] + pltpu.roll(v[:, half], 64, 1)).astype(jnp.bfloat16))
        return carry

    lax.fori_loop(0, 6, block, 0)


def kernel(lat_ref, pts_ref, tend_ref, traj_ref, coup_ref, waves_ref, out_ref, fine_ref, a_ref, b_ref, x_ref, x16_ref):
    tables(pts_ref, waves_ref, fine_ref, a_ref, b_ref)

    def piece_of(j):
        return jnp.concatenate([traj_ref[j].astype(jnp.float32), jnp.zeros((VARS, 48), jnp.float32)], axis=1)

    column(lat_ref, pts_ref, tend_ref, piece_of, coup_ref, x_ref)

    def put(d, value):
        out_ref[d] = value

    transform(x_ref, x16_ref, fine_ref, a_ref, b_ref, put)


def body(adjoint_tend, trajectory, coupling, row_lat, row_points, wave_order):
    tend = adjoint_tend[0, :, 0, :]
    traj = lax.all_gather(trajectory[:, 0, :], "col", axis=0)
    vmem = pl.BlockSpec(memory_space=pltpu.VMEM)
    smem = pl.BlockSpec(memory_space=pltpu.SMEM)
    parts = pl.pallas_call(
        kernel,
        out_shape=jax.ShapeDtypeStruct((BANDS, VARS, 128), jnp.bfloat16),
        in_specs=[smem, smem, vmem, vmem, vmem, vmem],
        out_specs=vmem,
        scratch_shapes=[
            pltpu.VMEM((FINE, LANES), jnp.bfloat16),
            pltpu.VMEM((24, LANES), jnp.float32),
            pltpu.VMEM((24, LANES), jnp.float32),
            pltpu.VMEM((COARSE, VARS, FINE), jnp.float32),
            pltpu.VMEM((COARSE * VARS, FINE), jnp.bfloat16),
        ],
        compiler_params=pltpu.CompilerParams(vmem_limit_bytes=32 << 20),
    )(row_lat, row_points, tend, traj, coupling, wave_order.reshape(1, -1))
    parts = lax.all_to_all(parts, "band", split_axis=0, concat_axis=0, tiled=True)
    parts = parts.reshape(BANDS, VARS, 2, OWN_WAVES)
    return parts.transpose(2, 1, 0, 3)[None]


def solution(mesh):
    return jax.shard_map(
        body,
        mesh=mesh,
        in_specs=(
            P("col", None, "band", None),
            P(None, "band", "col"),
            P(),
            P("band"),
            P("band"),
            P(),
        ),
        out_specs=P("col", None, None, None, "band"),
        check_vma=False,
    )
```

time: 334 us -> 303 us (0.907)
  blocking collectives: 17.7 us -> 295 us
  other arithmetic: 245 us -> 0 us
  starting transfers between devices: 41 us -> 0 us
  local copies, waits for them, and re-layouts: 19.7 us -> 1.56 us
  matrix products: 8.17 us -> 0 us
  Pallas kernels: 0 us -> 5.06 us
    all_gather x0 -> x1, blocking collectives: none -> 248 us  [body(): traj = lax.all_gather(trajectory[:, 0, :], 'col', axis=0)]
    another operation x3 -> x0, other arithmetic: 215 us -> none
    all_to_all x2 -> x0, starting transfers between devices: 41 us -> none  [the longest x1 24 us: body(): lax.all_to_all(adjoint_tend, 'col', split_axis=3, concat_axis=0, tiled=True)]
    all_to_all x1, blocking collectives: 17.7 us -> 46.9 us  [body(): lax.all_to_all(parts, 'band', split_axis=0, concat_axis=0, tiled=True)]
    unnamed x1 -> x0, other arithmetic: 28.9 us -> none
    unnamed x20 -> x6, local copies, waits for them, and re-layouts: 14 us -> 0.01 us
    dot_general x5 -> x0, matrix products: 8.17 us -> none  [the longest x3 5.67 us: body(): coeffs = jnp.dot(flat, table, preferred_element_type=jnp.float32) / root]
    pallas_call x0 -> x1, Pallas kernels: none -> 5.06 us  [body(): pl.pallas_call(kernel, out_shape=jax.ShapeDtypeStruct((BANDS, VARS, 128),...]
  transfers between devices with their start and end apart: 2 -> 0, of which waited for: 0 -> 0; matrix products, arithmetic and copies ran while one was open for 65% -> 0% of each run, Pallas kernels for 0% -> 0%
where the time goes in v1:
time: 303 us
  blocking collectives  295 us (97%)
  Pallas kernels  5.06 us (2%)
    all_gather x1, blocking collectives, body(): traj = lax.all_gather(trajectory[:, 0, :], 'col', axis=0)  248 us
    all_to_all x1, blocking collectives, body(): lax.all_to_all(parts, 'band', split_axis=0, concat_axis=0, tiled=True)  46.9 us

profile of v1, /device:TPU:1, one launch (start us, length us, event | category | flops | bytes accessed | tf_op | source)
XLA Modules:
  0.0 302.8 jit_solution(17817605099569822)
XLA Ops:
  0.0 0.0 copy-start.2
  0.0 0.0 copy-start
  1.4 0.7 reshape.6.waves_ref
  2.0 0.0 copy-done.2
  2.0 0.0 copy-start.1
  2.0 248.0 %all-gather = bf16[2560,1,80]{2,0,1:T(8,128)(2,1)S(1)} all-gather(bf16[40,1,80]{2,0,1:T(8,128)(2,1)S(1)} %copy-done.2), channel_id=2, replica_groups=mesh['band'=12,'col'=64] {'col'}, dimensions={0}, use_global_device_ids=true | all-gather | bytes 416000 | tf_op jit(solution)/shard_map/all_gather | solution.py:155
  250.0 0.0 copy-done
  250.0 0.0 copy-done.1
  250.0 5.1 %shard_map.64 = bf16[12,40,128]{2,1,0:T(8,128)(2,1)S(1)} custom-call(s32[1]{0:T(128)S(6)} %copy.10.lat_ref, s32[1]{0:T(128)S(6)} %copy.11.pts_ref, bf16[40,5120]{1,0:T(8,128)(2,1)S(1)} %bitcast.8, bf16[64,40,80]{2,1,0:T(8,128)(2,1)S(1)} %bitcast.7, bf16[40,40]{1,0:T(8,128)(2,1)S(1)} %copy-done.1, s32[1,768]{1,0:T(1,128)S(1)} %reshape.6.waves_ref), custom_call_target="tpu_custom_call" | custom-call | tf_op jit(solution)/shard_map/pallas_call | solution.py:158
  255.1 46.9 %all_to_all.5 = bf16[12,40,128]{2,1,0:T(8,128)(2,1)S(1)} all-to-all(bf16[12,40,128]{2,1,0:T(8,128)(2,1)S(1)} %shard_map.64), channel_id=1, replica_groups=mesh['band'=12,'col'=64] {'band'}, dimensions={0} | all-to-all | bytes 245760 | tf_op jit(solution)/shard_map/all_to_all | solution.py:172
  301.9 0.1 reshape.7
  302.1 0.7 copy.9
Async XLA Ops:
  0.0 2.0 copy-start.2
  0.0 250.0 %copy-start = (bf16[1,40,1,5120]{3,1,2,0:T(8,128)(2,1)S(1)}, bf16[1,40,1,5120]{3,1,2,0:T(8,128)(2,1)}, u32[]{:S(2)}) copy-start(bf16[1,40,1,5120]{3,1,2,0:T(8,128)(2,1)} %param.6) | copy-start | bytes 1228804
  2.0 248.0 %copy-start.1 = (bf16[40,40]{1,0:T(8,128)(2,1)S(1)}, bf16[40,40]{1,0:T(8,128)(2,1)}, u32[]{:S(2)}) copy-start(bf16[40,40]{1,0:T(8,128)(2,1)} %coup_ref.1) | copy-start | bytes 9604

commit v2 on v1

v2 whole, which is shorter than its diff:
```python
import jax
import jax.numpy as jnp
from jax import lax
from jax.experimental import pallas as pl
from jax.experimental.pallas import tpu as pltpu
from jax.sharding import PartitionSpec as P

LEVELS = 8
LATITUDES = 2560
VARS = 40
POINTS = 5120
WAVES = 768
PIECE = 80
MESH = pl.DeviceIdType.MESH
BANDS = 12
OWN_WAVES = 64
LANES = 2 * BANDS * OWN_WAVES
FINE = 256
COARSE = POINTS // FINE
SINE = (6.283185005187988, -41.34165573120117, 81.60100555419922, -76.5497817993164, 39.536705017089844)


def sine_turns(v):
    u = v * v
    p = jnp.full_like(u, SINE[-1])
    for c in SINE[-2::-1]:
        p = p * u + c
    return p * v


def cosine_turns(t):
    v = 0.25 - jnp.abs(t)
    return sine_turns(jnp.maximum(v, -0.5 - v))


def turns(pm, n, rn):
    q = jnp.floor(pm * rn + 0.5)
    return (pm - q * n) * rn


def tables(points, waves_ref, fine_ref, a_ref, b_ref, chosen):
    lane = lax.broadcasted_iota(jnp.int32, (8, 128), 1)
    first_half = lane < 64
    n8 = jnp.full((8, 128), points.astype(jnp.float32), jnp.float32)
    rn8 = 1.0 / n8
    root8 = 1.0 / jnp.sqrt(n8)
    shift8 = jnp.where(first_half, 0.0, 0.25)
    sign8 = jnp.where(first_half, 1.0, -1.0)
    row8 = lax.broadcasted_iota(jnp.int32, (8, 128), 0).astype(jnp.float32)
    for tile in chosen:
        pair = jnp.broadcast_to(waves_ref[pl.ds(128 * tile, 128)].reshape(1, 128), (8, 128)).astype(jnp.float32)
        turned = pltpu.roll(pair, 64, 1)
        for odd in range(2):
            w8 = jnp.where(first_half, pair, turned) if odd == 0 else jnp.where(first_half, turned, pair)
            at = (2 * tile + odd) * 128
            scale = jnp.where(2.0 * w8 < n8, root8, 0.0)
            for k in range(3):
                t = turns((row8 + 8.0 * k) * FINE * w8, n8, rn8)
                a_ref[8 * k : 8 * k + 8, at : at + 128] = scale * sign8 * cosine_turns(t)
                b_ref[8 * k : 8 * k + 8, at : at + 128] = -scale * cosine_turns(t - 0.25)
            wide = lambda v: jnp.broadcast_to(v[None], (FINE // 8, 8, 128)).reshape(FINE, 128)
            p0 = lax.broadcasted_iota(jnp.int32, (FINE, 128), 0).astype(jnp.float32)
            t = turns(p0 * wide(w8), wide(n8), wide(rn8))
            fine_ref[:, at : at + 128] = cosine_turns(t - wide(shift8)).astype(jnp.bfloat16)


def joined(pieces):
    lane = lax.broadcasted_iota(jnp.int32, (VARS, 128), 1)
    tiles = [None] * 5
    for j, piece in enumerate(pieces):
        tile, at = divmod(PIECE * j, 128)
        piece = jnp.concatenate([piece.astype(jnp.float32), jnp.zeros((VARS, 128 - PIECE), jnp.float32)], axis=1)
        turned = piece if at == 0 else pltpu.roll(piece, at, 1)
        tiles[tile] = turned if tiles[tile] is None else jnp.where(lane < at, tiles[tile], turned)
        if at + PIECE > 128:
            tiles[tile + 1] = turned
    return jnp.concatenate(tiles, axis=1).astype(jnp.bfloat16)


def column(latitude, points, tend_ref, traj_ref, coup_ref, x_ref, piece):
    ratio = (2.0 * jnp.full((8, 128), latitude.astype(jnp.float32)) + 1.0) / LATITUDES
    turning = jnp.tile(sine_turns(0.25 - 0.25 * ratio), (1, 5))
    coup = coup_ref[...]
    back = coup.astype(jnp.float32).T.astype(jnp.bfloat16)
    back2 = jnp.concatenate([back, back], axis=1)
    place = lax.broadcasted_iota(jnp.int32, (VARS, 640), 1)
    for half in range(2):
        at = (2 * piece + half) * 640
        traj16 = traj_ref[2 * piece + half]
        tend = tend_ref[:, pl.ds(pl.multiple_of(at, 128), 640)].astype(jnp.float32)
        driven = jnp.dot(coup, traj16, preferred_element_type=jnp.float32)
        weighted = tend * (1.0 + traj16.astype(jnp.float32))
        high = weighted.astype(jnp.bfloat16).astype(jnp.float32)
        both = jnp.concatenate([high, weighted - high], axis=0).astype(jnp.bfloat16)
        backed = jnp.dot(back2, both, preferred_element_type=jnp.float32)
        total = backed + tend * driven
        total = jnp.concatenate(
            [
                total[:LEVELS] - turning * tend[LEVELS : 2 * LEVELS],
                total[LEVELS : 2 * LEVELS] + turning * tend[:LEVELS],
                total[2 * LEVELS :],
            ],
            axis=0,
        )
        total = jnp.where(place < points - at, total, 0.0)
        for k in range(5):
            tile = 5 * half + k
            x_ref[5 * piece + tile // 2, :, 128 * (tile % 2) : 128 * (tile % 2) + 128] = total[:, 128 * k : 128 * k + 128]


def transform(x_ref, x16_ref, fine_ref, a_ref, b_ref, put):
    x16_ref[...] = x_ref[...].reshape(COARSE * VARS, FINE).astype(jnp.bfloat16)

    def block(j, carry):
        at = pl.multiple_of(j * 256, 256)
        y = jnp.dot(x16_ref[...], fine_ref[:, pl.ds(at, 256)], preferred_element_type=jnp.float32)
        u = jnp.zeros((VARS, 256), jnp.float32)
        v = jnp.zeros((VARS, 256), jnp.float32)
        for p1 in range(COARSE):
            part = y[VARS * p1 : VARS * (p1 + 1)]
            u = u + part * a_ref[p1 : p1 + 1, pl.ds(at, 256)]
            v = v + part * b_ref[p1 : p1 + 1, pl.ds(at, 256)]
        for odd in range(2):
            half = slice(128 * odd, 128 * odd + 128)
            put(2 * j + odd, (u[:, half] + pltpu.roll(v[:, half], 64, 1)).astype(jnp.bfloat16))
        return carry

    lax.fori_loop(0, 6, block, 0)


def kernel(
    tend_hbm, traj_hbm, coup_hbm, lat_hbm, pts_hbm, waves_hbm, out_ref,
    lat_ref, pts_ref, coup_ref, waves_ref, tend_ref, part_ref, line_ref, traj_ref, fine_ref, a_ref, b_ref, x_ref, x16_ref, send_ref,
    load_sem, own_sem, z_send, y_send, y_recv, x_send, x_recv, band_send, band_recv,
):
    band = lax.axis_index("band")
    col = lax.axis_index("col")
    x, y, z = col // 16, (col // 2) % 8, col % 2
    mine, other = 2 * y + z, 2 * y + 1 - z
    z_peer = (band, col + 1 - 2 * z)
    y_peers = [(band, 16 * x + 2 * ((y + s) % 8) + z) for s in range(1, 8)]
    x_peers = [(band, 16 * ((x + s) % 4) + 2 * y + z) for s in range(1, 4)]
    band_peers = [((band + s) % BANDS, col) for s in range(1, BANDS)]

    loads = [
        pltpu.make_async_copy(source, target, load_sem.at[i])
        for i, (source, target) in enumerate(
            [(pts_hbm, pts_ref), (waves_hbm, waves_ref), (lat_hbm, lat_ref), (coup_hbm, coup_ref), (tend_hbm, tend_ref)]
        )
    ]
    for load in loads:
        load.start()
    keep = pltpu.make_async_copy(traj_hbm, line_ref.at[mine], own_sem)
    keep.start()
    barrier = pltpu.get_barrier_semaphore()
    peers = [z_peer] + y_peers + x_peers + band_peers
    for peer in peers:
        pl.semaphore_signal(barrier, inc=1, device_id=peer, device_id_type=MESH)
    pl.semaphore_wait(barrier, len(peers))

    def to_line(source, slot, send_sem, peer):
        return pltpu.make_async_remote_copy(
            src_ref=source,
            dst_ref=line_ref.at[slot],
            send_sem=send_sem,
            recv_sem=y_recv.at[slot],
            device_id=peer,
            device_id_type=MESH,
        )

    across = to_line(traj_hbm, mine, z_send, z_peer)
    across.start()
    along = [to_line(traj_hbm, mine, y_send.at[0, s], peer) for s, peer in enumerate(y_peers)]
    for copy in along:
        copy.start()

    for load in loads[:2]:
        load.wait()
    points = pts_ref[0]
    tables(points, waves_ref, fine_ref, a_ref, b_ref, range(3))
    to_line(traj_hbm, other, z_send, z_peer).wait_recv()
    passed = [to_line(line_ref.at[other], other, y_send.at[1, s], peer) for s, peer in enumerate(y_peers)]
    for copy in passed:
        copy.start()
    tables(points, waves_ref, fine_ref, a_ref, b_ref, range(3, 6))
    keep.wait()
    for s in range(1, 8):
        for zz in range(2):
            to_line(traj_hbm, 2 * ((y + s) % 8) + zz, z_send, z_peer).wait_recv()

    spread = []
    for half in range(2):
        slot = 2 * x + half
        traj_ref[slot] = joined([line_ref[8 * half + j] for j in range(8)])
        for s, peer in enumerate(x_peers):
            copy = pltpu.make_async_remote_copy(
                src_ref=traj_ref.at[slot],
                dst_ref=traj_ref.at[slot],
                send_sem=x_send.at[half, s],
                recv_sem=x_recv.at[slot],
                device_id=peer,
                device_id_type=MESH,
            )
            copy.start()
            spread.append(copy)

    for load in loads[2:]:
        load.wait()
    for s in (0, 1, 3, 2):
        piece = (x + s) % 4
        if s > 0:
            for half in range(2):
                slot = 2 * piece + half
                pltpu.make_async_remote_copy(
                    src_ref=traj_ref.at[slot],
                    dst_ref=traj_ref.at[slot],
                    send_sem=x_send.at[half, 0],
                    recv_sem=x_recv.at[slot],
                    device_id=x_peers[0],
                    device_id_type=MESH,
                ).wait_recv()
        column(lat_ref[0], points, tend_ref, traj_ref, coup_ref, x_ref, piece)

    def put(d, value):
        send_ref[d] = value

    transform(x_ref, x16_ref, fine_ref, a_ref, b_ref, put)
    part_ref[band] = send_ref[band]

    def to_band(s, peer):
        return pltpu.make_async_remote_copy(
            src_ref=send_ref.at[peer[0]],
            dst_ref=part_ref.at[band],
            send_sem=band_send.at[s],
            recv_sem=band_recv.at[band],
            device_id=peer,
            device_id_type=MESH,
        )

    crossed = [to_band(s, peer) for s, peer in enumerate(band_peers)]
    for copy in crossed:
        copy.start()
    for s in range(1, BANDS):
        source = (band + s) % BANDS
        pltpu.make_async_remote_copy(
            src_ref=send_ref.at[source],
            dst_ref=part_ref.at[source],
            send_sem=band_send.at[0],
            recv_sem=band_recv.at[source],
            device_id=band_peers[0],
            device_id_type=MESH,
        ).wait_recv()
    for row in range(BANDS):
        both = part_ref[row].astype(jnp.float32)
        out_ref[0, row] = both[:, :OWN_WAVES].astype(jnp.bfloat16)
        out_ref[1, row] = both[:, OWN_WAVES:].astype(jnp.bfloat16)
    for copy in [across] + along + passed + spread + crossed:
        copy.wait_send()


def body(adjoint_tend, trajectory, coupling, row_lat, row_points, wave_order):
    vmem, smem, dma = pltpu.VMEM, pltpu.SMEM, pltpu.SemaphoreType.DMA
    spectra = pl.pallas_call(
        kernel,
        out_shape=jax.ShapeDtypeStruct((2, BANDS, VARS, OWN_WAVES), jnp.bfloat16),
        in_specs=[pl.BlockSpec(memory_space=pltpu.HBM)] * 6,
        out_specs=pl.BlockSpec(memory_space=vmem),
        scratch_shapes=[
            smem((1,), jnp.int32),
            smem((1,), jnp.int32),
            vmem((VARS, VARS), jnp.bfloat16),
            vmem((WAVES,), jnp.int32),
            vmem((VARS, POINTS), jnp.bfloat16),
            vmem((BANDS, VARS, 128), jnp.bfloat16),
            vmem((16, VARS, PIECE), jnp.bfloat16),
            vmem((8, VARS, 640), jnp.bfloat16),
            vmem((FINE, LANES), jnp.bfloat16),
            vmem((24, LANES), jnp.float32),
            vmem((24, LANES), jnp.float32),
            vmem((COARSE, VARS, FINE), jnp.float32),
            vmem((COARSE * VARS, FINE), jnp.bfloat16),
            vmem((BANDS, VARS, 128), jnp.bfloat16),
            dma((5,)),
            dma,
            dma,
            dma((2, 7)),
            dma((16,)),
            dma((2, 3)),
            dma((8,)),
            dma((BANDS - 1,)),
            dma((BANDS,)),
        ],
        compiler_params=pltpu.CompilerParams(
            vmem_limit_bytes=60 << 20, collective_id=0, has_side_effects=True
        ),
    )(adjoint_tend[0, :, 0, :], trajectory[:, 0, :], coupling, row_lat, row_points, wave_order)
    return spectra.transpose(0, 2, 1, 3)[None]


def solution(mesh):
    return jax.shard_map(
        body,
        mesh=mesh,
        in_specs=(
            P("col", None, "band", None),
            P(None, "band", "col"),
            P(),
            P("band"),
            P("band"),
            P(),
        ),
        out_specs=P("col", None, None, None, "band"),
        check_vma=False,
    )
```

time: 303 us -> 47.8 us (0.16)
  blocking collectives: 295 us -> 0 us
  Pallas kernels: 5.06 us -> 44.7 us
    all_gather x1 -> x0, blocking collectives: 248 us -> none  [body(): traj = lax.all_gather(trajectory[:, 0, :], 'col', axis=0)]
    all_to_all x1 -> x0, blocking collectives: 46.9 us -> none  [body(): lax.all_to_all(parts, 'band', split_axis=0, concat_axis=0, tiled=True)]
    pallas_call x1, Pallas kernels: 5.06 us -> 44.7 us  [body(): pl.pallas_call(kernel, out_shape=jax.ShapeDtypeStruct((2, BANDS, VARS, OW...]
where the time goes in v2:
time: 47.8 us; the launch traced here: 47.7 us
  Pallas kernels  44.7 us (94%)
  local copies, waits for them, and re-layouts  1.66 us (3%)
  between operations  1.3 us (3%)
    pallas_call x1, Pallas kernels, body(): pl.pallas_call(kernel, out_shape=jax.ShapeDtypeStruct((2, BANDS, VARS, OW...  44.7 us
    unnamed x1, local copies, waits for them, and re-layouts  1.66 us

profile of v2, /device:TPU:1, one launch (start us, length us, event | category | flops | bytes accessed | tf_op | source)
XLA Modules:
  0.0 47.7 jit_solution(1438976069448513697)
XLA Ops:
  1.3 44.7 %shard_map.64 = bf16[2,12,40,64]{3,2,1,0:T(8,128)(2,1)} custom-call(bf16[40,5120]{1,0:T(8,128)(2,1)} %bitcast.6, bf16[40,80]{1,0:T(8,128)(2,1)} %bitcast.7, bf16[40,40]{1,0:T(8,128)(2,1)} %coup_hbm.1, s32[1]{0:T(128)S(6)} %copy.8.lat_hbm, s32[1]{0:T(128)S(6)} %copy.9.pts_hbm, s32[768]{0:T(1024)} %waves_hbm.1), custom_call_target="tpu_custom_call" | custom-call | tf_op jit(solution)/shard_map/pallas_call | solution.py:263
  46.0 1.7 %copy.10 = bf16[1,2,40,12,64]{4,2,3,1,0:T(8,128)(2,1)} copy(bf16[1,2,40,12,64]{4,2,3,1,0:T(8,128)(2,1)} %bitcast.5) | data formatting | bytes 245760

commit v3 on v1

v3 whole, which is shorter than its diff:
```python
import jax
import jax.numpy as jnp
from jax import lax
from jax.experimental import pallas as pl
from jax.experimental.pallas import tpu as pltpu
from jax.sharding import PartitionSpec as P

LEVELS = 8
LATITUDES = 2560
VARS = 40
POINTS = 5120
WAVES = 768
PIECE = 80
BANDS = 12
OWN_WAVES = 64
LANES = 2 * BANDS * OWN_WAVES
STEP = 2 * PIECE
SINE = (6.283185005187988, -41.34165573120117, 81.60100555419922, -76.5497817993164, 39.536705017089844)
MESH = pl.DeviceIdType.MESH
NEAR_FIRST = (1, 7, 2, 6, 3, 5, 4)


def sine_turns(v):
    u = v * v
    p = jnp.full_like(u, SINE[-1])
    for c in SINE[-2::-1]:
        p = p * u + c
    return p * v


def cosine_turns(t):
    v = 0.25 - jnp.abs(t)
    return sine_turns(jnp.maximum(v, -0.5 - v))


def turns(pm, n, rn):
    q = jnp.floor(pm * rn + 0.5)
    return (pm - q * n) * rn


def tables(points, waves_ref, fine_ref, a_ref, b_ref, chosen):
    lane = lax.broadcasted_iota(jnp.int32, (8, 128), 1)
    first_half = lane < 64
    n8 = jnp.full((8, 128), points.astype(jnp.float32), jnp.float32)
    rn8 = 1.0 / n8
    root8 = 1.0 / jnp.sqrt(n8)
    shift8 = jnp.where(first_half, 0.0, 0.25)
    sign8 = jnp.where(first_half, 1.0, -1.0)
    row8 = lax.broadcasted_iota(jnp.int32, (8, 128), 0).astype(jnp.float32)
    for tile in chosen:
        pair = jnp.broadcast_to(waves_ref[pl.ds(128 * tile, 128)].reshape(1, 128), (8, 128)).astype(jnp.float32)
        turned = pltpu.roll(pair, 64, 1)
        for odd in range(2):
            w8 = jnp.where(first_half, pair, turned) if odd == 0 else jnp.where(first_half, turned, pair)
            at = (2 * tile + odd) * 128
            scale = jnp.where(2.0 * w8 < n8, root8, 0.0)
            for k in range(4):
                t = turns((row8 + 8.0 * k) * STEP * w8, n8, rn8)
                a_ref[8 * k : 8 * k + 8, at : at + 128] = scale * sign8 * cosine_turns(t)
                b_ref[8 * k : 8 * k + 8, at : at + 128] = -scale * cosine_turns(t - 0.25)
            wide = lambda v: jnp.broadcast_to(v[None], (PIECE // 8, 8, 128)).reshape(PIECE, 128)
            for zz in range(2):
                p0 = lax.broadcasted_iota(jnp.int32, (PIECE, 128), 0).astype(jnp.float32) + float(PIECE * zz)
                t = turns(p0 * wide(w8), wide(n8), wide(rn8))
                fine_ref[zz, 0:PIECE, at : at + 128] = cosine_turns(t - wide(shift8)).astype(jnp.bfloat16)


def repack(tend_ref, block_ref, xp):
    lane = lax.broadcasted_iota(jnp.int32, (VARS, 128), 1)
    for zz in range(2):
        for y in range(8):
            tile, at = divmod(STEP * y + PIECE * zz, 128)

            def load(k):
                start = pl.multiple_of(xp * 1280 + 128 * k, 128)
                return pltpu.roll(tend_ref[:, pl.ds(start, 128)].astype(jnp.float32), (128 - at) % 128, 1)

            piece = load(tile)
            if at + PIECE > 128:
                piece = jnp.where(lane < 128 - at, piece, load(tile + 1))
            block_ref[2 * xp + zz, :, 128 * y : 128 * y + 128] = piece


def column(turning, points, block_ref, piece_ref, coup_ref, back_ref, x_ref, xp, zz):
    zeros = jnp.zeros((VARS, 128 - PIECE), jnp.float32)
    pieces = [piece_ref[16 * xp + 2 * y + zz].astype(jnp.float32) for y in range(8)]
    traj = jnp.concatenate([part for piece in pieces for part in (piece, zeros)], axis=1)
    tend = block_ref[2 * xp + zz]
    driven = jnp.dot(coup_ref[...], traj.astype(jnp.bfloat16), preferred_element_type=jnp.float32)
    weighted = tend * (1.0 + traj)
    high = weighted.astype(jnp.bfloat16).astype(jnp.float32)
    both = jnp.concatenate([high, weighted - high], axis=0).astype(jnp.bfloat16)
    backed = jnp.dot(back_ref[...], both, preferred_element_type=jnp.float32)
    total = backed + tend * driven
    turn = jnp.tile(turning, (1, 8))
    total = jnp.concatenate(
        [
            total[:LEVELS] - turn * tend[LEVELS : 2 * LEVELS],
            total[LEVELS : 2 * LEVELS] + turn * tend[:LEVELS],
            total[2 * LEVELS :],
        ],
        axis=0,
    )
    q = lax.broadcasted_iota(jnp.int32, (VARS, 128), 1)
    first = xp * 1280 + zz * PIECE
    rows = []
    for y in range(8):
        keep = (q < PIECE) & (q + (first + STEP * y) < points)
        rows.append(jnp.where(keep, total[:, 128 * y : 128 * y + 128], 0.0))
    x_ref[...] = jnp.concatenate(rows, axis=0).astype(jnp.bfloat16)


def transform(x_ref, fine_ref, a_ref, b_ref, xp, zz, j):
    at = pl.multiple_of(j * 256, 256)
    y = jnp.dot(x_ref[...], fine_ref[zz, :, pl.ds(at, 256)], preferred_element_type=jnp.float32)
    a = a_ref[pl.ds(pl.multiple_of(8 * xp, 8), 8), pl.ds(at, 256)]
    b = b_ref[pl.ds(pl.multiple_of(8 * xp, 8), 8), pl.ds(at, 256)]
    u = y[:VARS] * a[0:1]
    v = y[:VARS] * b[0:1]
    for k in range(1, 8):
        part = y[VARS * k : VARS * (k + 1)]
        u = u + part * a[k : k + 1]
        v = v + part * b[k : k + 1]
    return u, v


def kernel(
    lat_ref, tend_hbm, traj_hbm, coup_hbm, waves_hbm, out_hbm,
    coup_ref, back_ref, waves_ref, tend_ref, block_ref, piece_ref,
    fine_ref, a_ref, b_ref, x_ref, u_ref, v_ref, send_ref,
    load_sem, own_sem, piece_recv, z_send, y_send, x_send, band_send, band_recv,
):
    band = lax.axis_index("band")
    col = lax.axis_index("col")
    x, y, z = col // 16, (col // 2) % 8, col % 2
    mate = col + 1 - 2 * z
    z_peer = (band, mate)
    y_peers = {s: (band, 16 * x + 2 * ((y + s) % 8) + z) for s in NEAR_FIRST}
    x_peers = [(band, 16 * ((x + s) % 4) + 2 * y + z) for s in (1, 3, 2)]
    band_peers = [((band + s) % BANDS, col) for s in range(1, BANDS)]

    loads = [
        pltpu.make_async_copy(source, target, load_sem.at[i])
        for i, (source, target) in enumerate(
            [(waves_hbm, waves_ref), (coup_hbm, coup_ref), (tend_hbm, tend_ref)]
        )
    ]
    for load in loads:
        load.start()
    keep = pltpu.make_async_copy(traj_hbm, piece_ref.at[col], own_sem)
    keep.start()
    barrier = pltpu.get_barrier_semaphore()
    peers = [z_peer] + list(y_peers.values()) + x_peers + band_peers
    for peer in peers:
        pl.semaphore_signal(barrier, inc=1, device_id=peer, device_id_type=MESH)
    pl.semaphore_wait(barrier, len(peers))

    sent = []

    def send(source, slot, send_sem, peer):
        copy = pltpu.make_async_remote_copy(
            src_ref=source,
            dst_ref=piece_ref.at[slot],
            send_sem=send_sem,
            recv_sem=piece_recv.at[slot],
            device_id=peer,
            device_id_type=MESH,
        )
        copy.start()
        sent.append(copy)

    def arrive(slot):
        pltpu.make_async_remote_copy(
            src_ref=piece_ref.at[slot],
            dst_ref=piece_ref.at[slot],
            send_sem=z_send,
            recv_sem=piece_recv.at[slot],
            device_id=z_peer,
            device_id_type=MESH,
        ).wait_recv()

    def along(source, slot, own):
        for s in NEAR_FIRST:
            send(source, slot, y_send.at[own, s], y_peers[s])

    def across(source, slot, own, s):
        for k, peer in enumerate(x_peers):
            send(source, slot, x_send.at[own, s, k], peer)

    send(traj_hbm, col, z_send, z_peer)
    along(traj_hbm, col, 0)
    across(traj_hbm, col, 0, 0)

    def pass_on(zz, own, offsets):
        for s in offsets:
            slot = 16 * x + 2 * ((y + s) % 8) + zz
            arrive(slot)
            across(piece_ref.at[slot], slot, own, s)

    loads[0].wait()
    latitude = lat_ref[0]
    points = jnp.minimum(20 + 4 * jnp.minimum(latitude, LATITUDES - 1 - latitude), POINTS)
    tables(points, waves_ref, fine_ref, a_ref, b_ref, range(3))
    pass_on(z, 0, NEAR_FIRST[:2])
    tables(points, waves_ref, fine_ref, a_ref, b_ref, range(3, 6))
    pass_on(z, 0, NEAR_FIRST[2:4])
    for load in loads[1:]:
        load.wait()
    ratio = (2.0 * jnp.full((8, 128), latitude.astype(jnp.float32)) + 1.0) / LATITUDES
    turning = sine_turns(0.25 - 0.25 * ratio)
    back = coup_ref[...].astype(jnp.float32).T.astype(jnp.bfloat16)
    back_ref[...] = jnp.concatenate([back, back], axis=1)
    for zz in range(2):
        fine_ref[zz, PIECE:] = jnp.zeros((128 - PIECE, LANES), jnp.bfloat16)
    pass_on(z, 0, NEAR_FIRST[4:])
    arrive(mate)
    along(piece_ref.at[mate], mate, 1)
    across(piece_ref.at[mate], mate, 1, 0)

    def two(xp, carry):
        repack(tend_ref, block_ref, xp)
        return carry

    lax.fori_loop(0, 4, two, 0)
    keep.wait()

    def add(xp, zz, first):
        column(turning, points, block_ref, piece_ref, coup_ref, back_ref, x_ref, xp, zz)

        def tile(j, carry):
            u, v = transform(x_ref, fine_ref, a_ref, b_ref, xp, zz, j)
            if not first:
                u = u + u_ref[j]
                v = v + v_ref[j]
            u_ref[j] = u
            v_ref[j] = v
            return carry

        lax.fori_loop(0, 6, tile, 0, unroll=True)

    def take(xp, zz):
        for k in range(8):
            arrive(16 * xp + 2 * k + zz)

    pass_on(1 - z, 1, NEAR_FIRST[:2])
    add(x, z, True)
    pass_on(1 - z, 1, NEAR_FIRST[2:])
    for s in (1, 3, 2):
        take((x + s) % 4, z)
        add((x + s) % 4, z, False)
    add(x, 1 - z, False)
    for s in (1, 3):
        take((x + s) % 4, 1 - z)
        add((x + s) % 4, 1 - z, False)

    xp, zz = (x + 2) % 4, 1 - z
    take(xp, zz)
    column(turning, points, block_ref, piece_ref, coup_ref, back_ref, x_ref, xp, zz)
    own = pltpu.make_async_copy(send_ref.at[band], out_hbm.at[band], own_sem)

    def to_band(d):
        return pltpu.make_async_remote_copy(
            src_ref=send_ref.at[d],
            dst_ref=out_hbm.at[band],
            send_sem=band_send.at[d],
            recv_sem=band_recv.at[band],
            device_id=(d, col),
            device_id_type=MESH,
        )

    def last(s, carry):
        j = jnp.where(band >= BANDS // 2, s, BANDS // 2 - 1 - s)
        u, v = transform(x_ref, fine_ref, a_ref, b_ref, xp, zz, j)
        u = u + u_ref[j]
        v = v + v_ref[j]
        for odd in range(2):
            d = 2 * j + odd
            half = slice(128 * odd, 128 * odd + 128)
            send_ref[d] = (u[:, half] + pltpu.roll(v[:, half], 64, 1)).astype(jnp.bfloat16)

            @pl.when(d != band)
            def _():
                to_band(d).start()

        return carry

    lax.fori_loop(0, 6, last, 0, unroll=True)
    own.start()
    for s in range(1, BANDS):
        source = (band + s) % BANDS
        pltpu.make_async_remote_copy(
            src_ref=send_ref.at[source],
            dst_ref=out_hbm.at[source],
            send_sem=band_send.at[source],
            recv_sem=band_recv.at[source],
            device_id=band_peers[0],
            device_id_type=MESH,
        ).wait_recv()
    own.wait()
    for copy in sent:
        copy.wait_send()
    for s in range(1, BANDS):
        to_band((band + s) % BANDS).wait_send()


def body(adjoint_tend, trajectory, coupling, row_lat, row_points, wave_order):
    vmem, smem, dma = pltpu.VMEM, pltpu.SMEM, pltpu.SemaphoreType.DMA
    arrays = [
        pltpu.with_memory_space_constraint(array, pltpu.HBM)
        for array in (adjoint_tend[0, :, 0, :], trajectory[:, 0, :], coupling, wave_order)
    ]
    parts = pl.pallas_call(
        kernel,
        out_shape=jax.ShapeDtypeStruct((BANDS, VARS, 128), jnp.bfloat16),
        in_specs=[pl.BlockSpec(memory_space=smem)] + [pl.BlockSpec(memory_space=pltpu.HBM)] * 4,
        out_specs=pl.BlockSpec(memory_space=vmem),
        scratch_shapes=[
            vmem((VARS, VARS), jnp.bfloat16),
            vmem((VARS, 2 * VARS), jnp.bfloat16),
            vmem((WAVES,), jnp.int32),
            vmem((VARS, POINTS), jnp.bfloat16),
            vmem((8, VARS, 1024), jnp.float32),
            vmem((64, VARS, PIECE), jnp.bfloat16),
            vmem((2, 128, LANES), jnp.bfloat16),
            vmem((32, LANES), jnp.float32),
            vmem((32, LANES), jnp.float32),
            vmem((8 * VARS, 128), jnp.bfloat16),
            vmem((6, VARS, 256), jnp.float32),
            vmem((6, VARS, 256), jnp.float32),
            vmem((BANDS, VARS, 128), jnp.bfloat16),
            dma((3,)),
            dma,
            dma((64,)),
            dma,
            dma((2, 8)),
            dma((2, 8, 3)),
            dma((BANDS,)),
            dma((BANDS,)),
        ],
        compiler_params=pltpu.CompilerParams(
            vmem_limit_bytes=32 << 20, collective_id=0, has_side_effects=True
        ),
    )(row_lat, *arrays)
    spectra = jnp.stack([parts[:, :, :OWN_WAVES], parts[:, :, OWN_WAVES:]])
    return spectra.transpose(0, 2, 1, 3)[None]


def solution(mesh):
    return jax.shard_map(
        body,
        mesh=mesh,
        in_specs=(
            P("col", None, "band", None),
            P(None, "band", "col"),
            P(),
            P("band"),
            P("band"),
            P(),
        ),
        out_specs=P("col", None, None, None, "band"),
        check_vma=False,
    )
```

time: 303 us -> 42.9 us (0.14)
  blocking collectives: 295 us -> 0 us
  Pallas kernels: 5.06 us -> 41.3 us
    all_gather x1 -> x0, blocking collectives: 248 us -> none  [body(): traj = lax.all_gather(trajectory[:, 0, :], 'col', axis=0)]
    all_to_all x1 -> x0, blocking collectives: 46.9 us -> none  [body(): lax.all_to_all(parts, 'band', split_axis=0, concat_axis=0, tiled=True)]
    pallas_call x1, Pallas kernels: 5.06 us -> 41.3 us  [body(): pl.pallas_call(kernel, out_shape=jax.ShapeDtypeStruct((BANDS, VARS, 128),...]
where the time goes in v3:
time: 42.9 us; the launch traced here: 42.8 us
  Pallas kernels  41.3 us (96%)
  other arithmetic  0.75 us (2%)
  between operations  0.66 us (2%)
    pallas_call x1, Pallas kernels, body(): pl.pallas_call(kernel, out_shape=jax.ShapeDtypeStruct((BANDS, VARS, 128),...  41.3 us

profile of v3, /device:TPU:1, one launch (start us, length us, event | category | flops | bytes accessed | tf_op | source)
XLA Modules:
  0.0 42.8 jit_solution(4999101650621098748)
XLA Ops:
  0.7 41.3 %shard_map.55 = bf16[12,40,128]{2,1,0:T(8,128)(2,1)S(1)} custom-call(s32[1]{0:T(128)S(6)} %copy.6.lat_ref, bf16[40,5120]{1,0:T(8,128)(2,1)} %bitcast.10, bf16[40,80]{1,0:T(8,128)(2,1)} %bitcast.11, bf16[40,40]{1,0:T(8,128)(2,1)} %coup_hbm.1, s32[768]{0:T(1024)} %waves_hbm.1), custom_call_target="tpu_custom_call" | custom-call | tf_op jit(solution)/shard_map/pallas_call | solution.py:312
  41.9 0.1 slice_bitcast_fusion.1
  42.0 0.7 %maximum_bitcast_fusion = bf16[1,2,40,12,64]{4,2,3,1,0:T(8,128)(2,1)} fusion(bf16[1,12,40,64]{3,2,1,0:T(8,128)(2,1)S(1)} %get-tuple-element.6, bf16[1,12,40,64]{3,2,1,0:T(8,128)(2,1)S(1)} %get-tuple-element.5), kind=kLoop, calls=%fused_computation | loop fusion | flops 61440 | bytes 245760 | tf_op jit(solution)/shard_map/broadcast_in_dim | solution.py:345

commit v4 on v3

--- a/solution.py
+++ b/solution.py
@@ -128,7 +128,7 @@
     lat_ref, tend_hbm, traj_hbm, coup_hbm, waves_hbm, out_hbm,
     coup_ref, back_ref, waves_ref, tend_ref, block_ref, piece_ref,
     fine_ref, a_ref, b_ref, x_ref, u_ref, v_ref, send_ref,
-    load_sem, own_sem, piece_recv, z_send, y_send, x_send, band_send, band_recv,
+    load_sem, own_sem, piece_recv, z_send, y_send, x_send, band_send, band_recv, known,
 ):
     band = lax.axis_index("band")
     col = lax.axis_index("col")
@@ -150,10 +150,30 @@
     keep = pltpu.make_async_copy(traj_hbm, piece_ref.at[col], own_sem)
     keep.start()
     barrier = pltpu.get_barrier_semaphore()
-    peers = [z_peer] + list(y_peers.values()) + x_peers + band_peers
-    for peer in peers:
-        pl.semaphore_signal(barrier, inc=1, device_id=peer, device_id_type=MESH)
-    pl.semaphore_wait(barrier, len(peers))
+    level = band // 2
+
+    def near(step, act):
+        for sign in (-1, 1):
+
+            @pl.when((level + sign * step >= 0) & (level + sign * step < BANDS // 2))
+            def _():
+                act((band + 2 * sign * step, col))
+
+    def beside(step):
+        return jnp.where(level >= step, 1, 0) + jnp.where(level < BANDS // 2 - step, 1, 0)
+
+    def call(semaphore, peer):
+        pl.semaphore_signal(semaphore, inc=1, device_id=peer, device_id_type=MESH)
+
+    core_peer = (band + 1 - 2 * (band % 2), col)
+    @pl.when(z == 0)
+    def _():
+        call(barrier, z_peer)
+
+    for peer in list(y_peers.values()) + x_peers + [core_peer]:
+        call(barrier, peer)
+    near(1, lambda peer: call(barrier, peer))
+    pl.semaphore_wait(barrier, 11 + beside(1) + z)
 
     sent = []
 
@@ -187,9 +207,23 @@
         for k, peer in enumerate(x_peers):
             send(source, slot, x_send.at[own, s, k], peer)
 
-    send(traj_hbm, col, z_send, z_peer)
+    exchange = pltpu.make_async_remote_copy(
+        src_ref=traj_hbm,
+        dst_ref=piece_ref.at[col],
+        send_sem=z_send,
+        recv_sem=piece_recv.at[col],
+        device_id=z_peer,
+        device_id_type=MESH,
+    )
+    sent.append(exchange)
+
+    @pl.when(z == 1)
+    def _():
+        exchange.start()
+
     along(traj_hbm, col, 0)
     across(traj_hbm, col, 0, 0)
+    near(1, lambda peer: call(known.at[0], peer))
 
     def pass_on(zz, own, offsets):
         for s in offsets:
@@ -202,6 +236,8 @@
     points = jnp.minimum(20 + 4 * jnp.minimum(latitude, LATITUDES - 1 - latitude), POINTS)
     tables(points, waves_ref, fine_ref, a_ref, b_ref, range(3))
     pass_on(z, 0, NEAR_FIRST[:2])
+    pl.semaphore_wait(known.at[0], beside(1))
+    near(2, lambda peer: call(known.at[1], peer))
     tables(points, waves_ref, fine_ref, a_ref, b_ref, range(3, 6))
     pass_on(z, 0, NEAR_FIRST[2:4])
     for load in loads[1:]:
@@ -213,7 +249,14 @@
     for zz in range(2):
         fine_ref[zz, PIECE:] = jnp.zeros((128 - PIECE, LANES), jnp.bfloat16)
     pass_on(z, 0, NEAR_FIRST[4:])
+    pl.semaphore_wait(known.at[1], beside(2))
+    near(1, lambda peer: call(known.at[2], peer))
     arrive(mate)
+
+    @pl.when(z == 0)
+    def _():
+        exchange.start()
+
     along(piece_ref.at[mate], mate, 1)
     across(piece_ref.at[mate], mate, 1, 0)
 
@@ -222,6 +265,8 @@
         return carry
 
     lax.fori_loop(0, 4, two, 0)
+    pl.semaphore_wait(known.at[2], beside(1))
+    call(known.at[3], core_peer)
     keep.wait()
 
     def add(xp, zz, first):
@@ -253,6 +298,7 @@
         take((x + s) % 4, 1 - z)
         add((x + s) % 4, 1 - z, False)
 
+    pl.semaphore_wait(known.at[3], 1)
     xp, zz = (x + 2) % 4, 1 - z
     take(xp, zz)
     column(turning, points, block_ref, piece_ref, coup_ref, back_ref, x_ref, xp, zz)
@@ -336,6 +382,7 @@
             dma((2, 8, 3)),
             dma((BANDS,)),
             dma((BANDS,)),
+            pltpu.SemaphoreType.REGULAR((4,)),
         ],
         compiler_params=pltpu.CompilerParams(
             vmem_limit_bytes=32 << 20, collective_id=0, has_side_effects=True

time: 42.9 us -> 42.1 us (0.981)
  Pallas kernels: 41.3 us -> 40.4 us
    pallas_call x1, Pallas kernels: 41.3 us -> 40.4 us  [body(): pl.pallas_call(kernel, out_shape=jax.ShapeDtypeStruct((BANDS, VARS, 128),...]
where the time goes in v4:
time: 42.1 us; the launch traced here: 42 us
  Pallas kernels  40.4 us (96%)
  other arithmetic  0.75 us (2%)
  between operations  0.66 us (2%)
    pallas_call x1, Pallas kernels, body(): pl.pallas_call(kernel, out_shape=jax.ShapeDtypeStruct((BANDS, VARS, 128),...  40.4 us

profile of v4, /device:TPU:1, one launch (start us, length us, event | category | flops | bytes accessed | tf_op | source)
XLA Modules:
  0.0 42.0 jit_solution(16499057391883634055)
XLA Ops:
  0.7 40.4 %shard_map.55 = bf16[12,40,128]{2,1,0:T(8,128)(2,1)S(1)} custom-call(s32[1]{0:T(128)S(6)} %copy.6.lat_ref, bf16[40,5120]{1,0:T(8,128)(2,1)} %bitcast.10, bf16[40,80]{1,0:T(8,128)(2,1)} %bitcast.11, bf16[40,40]{1,0:T(8,128)(2,1)} %coup_hbm.1, s32[768]{0:T(1024)} %waves_hbm.1), custom_call_target="tpu_custom_call" | custom-call | tf_op jit(solution)/shard_map/pallas_call | solution.py:358
  41.1 0.1 slice_bitcast_fusion.1
  41.2 0.7 %maximum_bitcast_fusion = bf16[1,2,40,12,64]{4,2,3,1,0:T(8,128)(2,1)} fusion(bf16[1,12,40,64]{3,2,1,0:T(8,128)(2,1)S(1)} %get-tuple-element.6, bf16[1,12,40,64]{3,2,1,0:T(8,128)(2,1)S(1)} %get-tuple-element.5), kind=kLoop, calls=%fused_computation | loop fusion | flops 61440 | bytes 245760 | tf_op jit(solution)/shard_map/broadcast_in_dim | solution.py:392

commit v5 on v4

--- a/solution.py
+++ b/solution.py
@@ -125,9 +125,9 @@
 
 
 def kernel(
-    lat_ref, tend_hbm, traj_hbm, coup_hbm, waves_hbm, out_hbm,
+    lat_ref, tend_hbm, traj_hbm, coup_hbm, waves_hbm, out_ref,
     coup_ref, back_ref, waves_ref, tend_ref, block_ref, piece_ref,
-    fine_ref, a_ref, b_ref, x_ref, u_ref, v_ref, send_ref,
+    fine_ref, a_ref, b_ref, x_ref, u_ref, v_ref, send_ref, part_ref,
     load_sem, own_sem, piece_recv, z_send, y_send, x_send, band_send, band_recv, known,
 ):
     band = lax.axis_index("band")
@@ -139,6 +139,30 @@
     x_peers = [(band, 16 * ((x + s) % 4) + 2 * y + z) for s in (1, 3, 2)]
     band_peers = [((band + s) % BANDS, col) for s in range(1, BANDS)]
 
+    barrier = pltpu.get_barrier_semaphore()
+    level = band // 2
+
+    def near(step, act):
+        for sign in (-1, 1):
+
+            @pl.when((level + sign * step >= 0) & (level + sign * step < BANDS // 2))
+            def _():
+                act((band + 2 * sign * step, col))
+
+    def beside(step):
+        return jnp.where(level >= step, 1, 0) + jnp.where(level < BANDS // 2 - step, 1, 0)
+
+    def call(semaphore, peer):
+        pl.semaphore_signal(semaphore, inc=1, device_id=peer, device_id_type=MESH)
+
+    core_peer = (band + 1 - 2 * (band % 2), col)
+    @pl.when(z == 0)
+    def _():
+        call(barrier, z_peer)
+
+    for peer in list(y_peers.values()) + x_peers + [core_peer]:
+        call(barrier, peer)
+    near(1, lambda peer: call(barrier, peer))
     loads = [
         pltpu.make_async_copy(source, target, load_sem.at[i])
         for i, (source, target) in enumerate(
@@ -149,30 +173,6 @@
         load.start()
     keep = pltpu.make_async_copy(traj_hbm, piece_ref.at[col], own_sem)
     keep.start()
-    barrier = pltpu.get_barrier_semaphore()
-    level = band // 2
-
-    def near(step, act):
-        for sign in (-1, 1):
-
-            @pl.when((level + sign * step >= 0) & (level + sign * step < BANDS // 2))
-            def _():
-                act((band + 2 * sign * step, col))
-
-    def beside(step):
-        return jnp.where(level >= step, 1, 0) + jnp.where(level < BANDS // 2 - step, 1, 0)
-
-    def call(semaphore, peer):
-        pl.semaphore_signal(semaphore, inc=1, device_id=peer, device_id_type=MESH)
-
-    core_peer = (band + 1 - 2 * (band % 2), col)
-    @pl.when(z == 0)
-    def _():
-        call(barrier, z_peer)
-
-    for peer in list(y_peers.values()) + x_peers + [core_peer]:
-        call(barrier, peer)
-    near(1, lambda peer: call(barrier, peer))
     pl.semaphore_wait(barrier, 11 + beside(1) + z)
 
     sent = []
@@ -248,25 +248,12 @@
     back_ref[...] = jnp.concatenate([back, back], axis=1)
     for zz in range(2):
         fine_ref[zz, PIECE:] = jnp.zeros((128 - PIECE, LANES), jnp.bfloat16)
-    pass_on(z, 0, NEAR_FIRST[4:])
-    pl.semaphore_wait(known.at[1], beside(2))
-    near(1, lambda peer: call(known.at[2], peer))
-    arrive(mate)
-
-    @pl.when(z == 0)
-    def _():
-        exchange.start()
-
-    along(piece_ref.at[mate], mate, 1)
-    across(piece_ref.at[mate], mate, 1, 0)
 
     def two(xp, carry):
         repack(tend_ref, block_ref, xp)
         return carry
 
     lax.fori_loop(0, 4, two, 0)
-    pl.semaphore_wait(known.at[2], beside(1))
-    call(known.at[3], core_peer)
     keep.wait()
 
     def add(xp, zz, first):
@@ -287,12 +274,28 @@
         for k in range(8):
             arrive(16 * xp + 2 * k + zz)
 
-    pass_on(1 - z, 1, NEAR_FIRST[:2])
+    pass_on(z, 0, NEAR_FIRST[4:])
+    pl.semaphore_wait(known.at[1], beside(2))
+    near(1, lambda peer: call(known.at[2], peer))
     add(x, z, True)
-    pass_on(1 - z, 1, NEAR_FIRST[2:])
-    for s in (1, 3, 2):
-        take((x + s) % 4, z)
-        add((x + s) % 4, z, False)
+    arrive(mate)
+
+    @pl.when(z == 0)
+    def _():
+        exchange.start()
+
+    along(piece_ref.at[mate], mate, 1)
+    across(piece_ref.at[mate], mate, 1, 0)
+
+    take((x + 1) % 4, z)
+    add((x + 1) % 4, z, False)
+    take((x + 3) % 4, z)
+    add((x + 3) % 4, z, False)
+    take((x + 2) % 4, z)
+    add((x + 2) % 4, z, False)
+    pl.semaphore_wait(known.at[2], beside(1))
+    call(known.at[3], core_peer)
+    pass_on(1 - z, 1, NEAR_FIRST[:])
     add(x, 1 - z, False)
     for s in (1, 3):
         take((x + s) % 4, 1 - z)
@@ -302,12 +305,17 @@
     xp, zz = (x + 2) % 4, 1 - z
     take(xp, zz)
     column(turning, points, block_ref, piece_ref, coup_ref, back_ref, x_ref, xp, zz)
-    own = pltpu.make_async_copy(send_ref.at[band], out_hbm.at[band], own_sem)
+
+    def unpack(row, ref):
+        both = ref[row].astype(jnp.float32)
+        out_ref[0, row] = both[:, :OWN_WAVES].astype(jnp.bfloat16)
+        out_ref[1, row] = both[:, OWN_WAVES:].astype(jnp.bfloat16)
+
 
     def to_band(d):
         return pltpu.make_async_remote_copy(
             src_ref=send_ref.at[d],
-            dst_ref=out_hbm.at[band],
+            dst_ref=part_ref.at[band],
             send_sem=band_send.at[d],
             recv_sem=band_recv.at[band],
             device_id=(d, col),
@@ -331,20 +339,20 @@
         return carry
 
     lax.fori_loop(0, 6, last, 0, unroll=True)
-    own.start()
+    unpack(band, send_ref)
+    for copy in sent:
+        copy.wait_send()
     for s in range(1, BANDS):
         source = (band + s) % BANDS
         pltpu.make_async_remote_copy(
             src_ref=send_ref.at[source],
-            dst_ref=out_hbm.at[source],
+            dst_ref=part_ref.at[source],
             send_sem=band_send.at[source],
             recv_sem=band_recv.at[source],
             device_id=band_peers[0],
             device_id_type=MESH,
         ).wait_recv()
-    own.wait()
-    for copy in sent:
-        copy.wait_send()
+        unpack(source, part_ref)
     for s in range(1, BANDS):
         to_band((band + s) % BANDS).wait_send()
 
@@ -357,7 +365,7 @@
     ]
     parts = pl.pallas_call(
         kernel,
-        out_shape=jax.ShapeDtypeStruct((BANDS, VARS, 128), jnp.bfloat16),
+        out_shape=jax.ShapeDtypeStruct((2, BANDS, VARS, OWN_WAVES), jnp.bfloat16),
         in_specs=[pl.BlockSpec(memory_space=smem)] + [pl.BlockSpec(memory_space=pltpu.HBM)] * 4,
         out_specs=pl.BlockSpec(memory_space=vmem),
         scratch_shapes=[
@@ -374,6 +382,7 @@
             vmem((6, VARS, 256), jnp.float32),
             vmem((6, VARS, 256), jnp.float32),
             vmem((BANDS, VARS, 128), jnp.bfloat16),
+            vmem((BANDS, VARS, 128), jnp.bfloat16),
             dma((3,)),
             dma,
             dma((64,)),
@@ -388,8 +397,7 @@
             vmem_limit_bytes=32 << 20, collective_id=0, has_side_effects=True
         ),
     )(row_lat, *arrays)
-    spectra = jnp.stack([parts[:, :, :OWN_WAVES], parts[:, :, OWN_WAVES:]])
-    return spectra.transpose(0, 2, 1, 3)[None]
+    return parts.transpose(0, 2, 1, 3)[None]
 
 
 def solution(mesh):

time: 42.1 us -> 41.9 us (level)
  other arithmetic: 0.75 us -> 0 us
  local copies, waits for them, and re-layouts: 0.11 us -> 0.7 us
    broadcast_in_dim x1 -> x0, other arithmetic: 0.75 us -> none  [body(): return spectra.transpose(0, 2, 1, 3)[None]]
    unnamed x0 -> x1, local copies, waits for them, and re-layouts: none -> 0.7 us
where the time goes in v5:
time: 41.9 us; the launch traced here: 41.8 us
  Pallas kernels  40.4 us (96%)
  local copies, waits for them, and re-layouts  0.7 us (2%)
  between operations  0.66 us (2%)
    pallas_call x1, Pallas kernels, body(): pl.pallas_call(kernel, out_shape=jax.ShapeDtypeStruct((2, BANDS, VARS, OW...  40.4 us

profile of v5, /device:TPU:1, one launch (start us, length us, event | category | flops | bytes accessed | tf_op | source)
XLA Modules:
  0.0 41.8 jit_solution(208743790010092486)
XLA Ops:
  0.7 40.4 %shard_map.55 = bf16[2,12,40,64]{3,2,1,0:T(8,128)(2,1)S(1)} custom-call(s32[1]{0:T(128)S(6)} %copy.7.lat_ref, bf16[40,5120]{1,0:T(8,128)(2,1)} %bitcast.6, bf16[40,80]{1,0:T(8,128)(2,1)} %bitcast.7, bf16[40,40]{1,0:T(8,128)(2,1)} %coup_hbm.1, s32[768]{0:T(1024)} %waves_hbm.1), custom_call_target="tpu_custom_call" | custom-call | tf_op jit(solution)/shard_map/pallas_call | solution.py:366
  41.1 0.7 %copy.8 = bf16[1,2,40,12,64]{4,2,3,1,0:T(8,128)(2,1)} copy(bf16[1,2,40,12,64]{4,2,3,1,0:T(8,128)(2,1)S(1)} %bitcast.5) | data formatting | bytes 245760

commit v6 on v5

--- a/solution.py
+++ b/solution.py
@@ -200,7 +200,7 @@
         ).wait_recv()
 
     def along(source, slot, own):
-        for s in NEAR_FIRST:
+        for s in (1, 7, 4, 2, 6, 3, 5):
             send(source, slot, y_send.at[own, s], y_peers[s])
 
     def across(source, slot, own, s):
@@ -279,13 +279,13 @@
     near(1, lambda peer: call(known.at[2], peer))
     add(x, z, True)
     arrive(mate)
+    along(piece_ref.at[mate], mate, 1)
+    across(piece_ref.at[mate], mate, 1, 0)
 
     @pl.when(z == 0)
     def _():
         exchange.start()
 
-    along(piece_ref.at[mate], mate, 1)
-    across(piece_ref.at[mate], mate, 1, 0)
 
     take((x + 1) % 4, z)
     add((x + 1) % 4, z, False)

time: 41.9 us -> 41.9 us (level)
  no operation moved by 1% of the time
where the time goes in v6:
time: 41.9 us; the launch traced here: 41.8 us
  Pallas kernels  40.4 us (96%)
  local copies, waits for them, and re-layouts  0.7 us (2%)
  between operations  0.66 us (2%)
    pallas_call x1, Pallas kernels, body(): pl.pallas_call(kernel, out_shape=jax.ShapeDtypeStruct((2, BANDS, VARS, OW...  40.4 us

profile of v6, /device:TPU:1, one launch (start us, length us, event | category | flops | bytes accessed | tf_op | source)
XLA Modules:
  0.0 41.8 jit_solution(6303161933886764824)
XLA Ops:
  0.7 40.4 %shard_map.55 = bf16[2,12,40,64]{3,2,1,0:T(8,128)(2,1)S(1)} custom-call(s32[1]{0:T(128)S(6)} %copy.7.lat_ref, bf16[40,5120]{1,0:T(8,128)(2,1)} %bitcast.6, bf16[40,80]{1,0:T(8,128)(2,1)} %bitcast.7, bf16[40,40]{1,0:T(8,128)(2,1)} %coup_hbm.1, s32[768]{0:T(1024)} %waves_hbm.1), custom_call_target="tpu_custom_call" | custom-call | tf_op jit(solution)/shard_map/pallas_call | solution.py:366
  41.1 0.7 %copy.8 = bf16[1,2,40,12,64]{4,2,3,1,0:T(8,128)(2,1)} copy(bf16[1,2,40,12,64]{4,2,3,1,0:T(8,128)(2,1)S(1)} %bitcast.5) | data formatting | bytes 245760

commit v7 on v6

--- a/solution.py
+++ b/solution.py
@@ -136,7 +136,7 @@
     mate = col + 1 - 2 * z
     z_peer = (band, mate)
     y_peers = {s: (band, 16 * x + 2 * ((y + s) % 8) + z) for s in NEAR_FIRST}
-    x_peers = [(band, 16 * ((x + s) % 4) + 2 * y + z) for s in (1, 3, 2)]
+    x_peers = [(band, 16 * ((x + s) % 4) + 2 * y + z) for s in (2, 1, 3)]
     band_peers = [((band + s) % BANDS, col) for s in range(1, BANDS)]
 
     barrier = pltpu.get_barrier_semaphore()

time: 41.9 us -> 41.9 us (level)
  no operation moved by 1% of the time
where the time goes in v7:
time: 41.9 us; the launch traced here: 41.7 us
  Pallas kernels  40.4 us (96%)
  local copies, waits for them, and re-layouts  0.7 us (2%)
  between operations  0.66 us (2%)
    pallas_call x1, Pallas kernels, body(): pl.pallas_call(kernel, out_shape=jax.ShapeDtypeStruct((2, BANDS, VARS, OW...  40.4 us

profile of v7, /device:TPU:1, one launch (start us, length us, event | category | flops | bytes accessed | tf_op | source)
XLA Modules:
  0.0 41.7 jit_solution(3133748862413491935)
XLA Ops:
  0.7 40.4 %shard_map.55 = bf16[2,12,40,64]{3,2,1,0:T(8,128)(2,1)S(1)} custom-call(s32[1]{0:T(128)S(6)} %copy.7.lat_ref, bf16[40,5120]{1,0:T(8,128)(2,1)} %bitcast.6, bf16[40,80]{1,0:T(8,128)(2,1)} %bitcast.7, bf16[40,40]{1,0:T(8,128)(2,1)} %coup_hbm.1, s32[768]{0:T(1024)} %waves_hbm.1), custom_call_target="tpu_custom_call" | custom-call | tf_op jit(solution)/shard_map/pallas_call | solution.py:366
  41.0 0.7 %copy.8 = bf16[1,2,40,12,64]{4,2,3,1,0:T(8,128)(2,1)} copy(bf16[1,2,40,12,64]{4,2,3,1,0:T(8,128)(2,1)S(1)} %bitcast.5) | data formatting | bytes 245760
